TPU v7x, 256 devices: a whole 4x4x8 slice. The times are simulated.
256 devices in a mesh: seq: 32 (over y, x, core), tp: 8 (over z).
Axes of the slice: x: 4, y: 4, z: 8, core: 2. Of those that a mesh axis runs over, the one named last changes fastest.
Arguments:
- queries: bfloat16 [32, 64, 4096], P('seq', None, 'tp'), may hold values from -8 to 8
- draft_kv: bfloat16 [32, 64, 8, 128], P('seq', None, 'tp'), may hold values from -12.5 to 12.5
- cache_kv: bfloat16 [8, 16384, 8, 128], P(None, 'seq', 'tp'), may hold values from -10 to 10
- cache_len: int32 [8], replicated, may hold values from 4096 to 16384
- group_of: int32 [32], replicated, may hold values from 0 to 7, as said below
- parents: int32 [32, 64], P('seq'), may hold values from 0 to 62, as said below
- sink_logit: float32 [64], P('tp'), may hold values from 4 to 20
- w_out: bfloat16 [4096, 2880], P('tp'), may hold values from -0.09375 to 0.09375
- hidden_in: bfloat16 [2048, 2880], P('seq', 'tp'), may hold values from -3 to 3
- norm_gain: float32 [2880], replicated, may hold values from 0.5 to 1.5
- routes: int32 [2048, 4], P('seq'), may hold values from 0 to 31, all different within a row; in each aligned block of 64 rows (0 to 63, 64 to 127, ...) at most 16 rows name the same one
- route_weight: float32 [2048, 4], P('seq'), may hold values from 0.1 to 1
- w_gate_up: bfloat16 [32, 2, 2880, 2880], P('seq', None, None, 'tp'), may hold values from -0.109375 to 0.109375
- w_down: bfloat16 [32, 2880, 2880], P('seq', 'tp'), may hold values from -0.109375 to 0.109375
- accepted_idx: int32 [32, 16], P('seq'), may hold values from 0 to 45, as said below
- accepted_len: int32 [32], P('seq'), may hold values from 1 to 16, as said below
- tail_slot: int32 [32], replicated, may hold values from 0 to 31, each once
Outputs:
- out_hidden: bfloat16 [2048, 2880], P('seq', 'tp')
- new_tail: bfloat16 [32, 16, 8, 128], P('seq', None, 'tp')
Inputs may be any that keep to these rules, and one draw needn't show every extreme that they name: `parents`: node 0 of every tree is its root and its own parent; every other node's parent is one of the three nodes before it. `accepted_idx`: row r lists the first 16 nodes of a path from the root of request r's tree down to one of its last four nodes, root first. `accepted_len`: each request accepts one or more nodes. `group_of`: every prompt group has exactly 4 requests. `routes`: the 4 experts of a token differ; at most 16 of one device's rows (one aligned block of 64 tokens) name one expert.
All inputs are finite; a program needn't handle non-finite values.
Results may differ from a plain program's by a relative error of at most 0.025.
Values may be sent and summed in bfloat16 or wider, within the bound.
A program may use at most 128 MiB of HBM per device.

v0:
```python
import jax
import jax.numpy as jnp
from jax import lax
from jax.sharding import PartitionSpec as P

HQ = 64
KVH = 8
HD = 64


def ancestry(parents):
    tree_len = parents.shape[1]
    node_ids = jnp.arange(tree_len, dtype=jnp.int32)
    linked = (parents[:, :, None] == node_ids[None, None, :]) | (
        node_ids[:, None] == node_ids[None, :]
    )[None]
    reachable = linked.astype(jnp.float32)
    for repeat in range((tree_len - 1).bit_length()):
        reachable = jnp.minimum(
            jnp.einsum("rij,rjk->rik", reachable, reachable, precision=lax.Precision.HIGHEST), 1.0
        )
    return reachable


def cache_block(block_queries, block_groups, cache_kv, cache_len, positions):
    block_rows, tree_len, head_cols = block_queries.shape
    kv_dev = cache_kv.shape[2]
    grouped = block_queries.reshape(block_rows, tree_len, kv_dev, HQ // KVH, HD)
    picked = jnp.take(cache_kv, block_groups, axis=0)
    cache_keys = picked[..., :HD]
    cache_values = picked[..., HD:]
    scores = (
        jnp.einsum("rtkqd,rckd->rkqtc", grouped, cache_keys, preferred_element_type=jnp.float32)
        * 0.125
    )
    lengths = jnp.take(cache_len, block_groups)
    usable = (positions[None, :] < lengths[:, None])[:, None, None, None, :]
    masked = jnp.where(usable, scores, -1e30)
    shard_max = jnp.max(masked, axis=-1)
    weights = jnp.where(usable, jnp.exp(masked - shard_max[..., None]), 0.0)
    shard_sum = jnp.sum(weights, axis=-1)
    shard_out = jnp.einsum(
        "rkqtc,rckd->rkqtd",
        weights.astype(jnp.bfloat16),
        cache_values,
        preferred_element_type=jnp.float32,
    )
    shard_out = (shard_out / jnp.maximum(shard_sum, 1.0)[..., None]).astype(jnp.bfloat16)
    out_rows = shard_out.transpose(0, 3, 1, 2, 4).reshape(block_rows, tree_len, head_cols)
    max_rows = shard_max.transpose(0, 3, 1, 2).reshape(block_rows, tree_len, -1)
    sum_rows = shard_sum.transpose(0, 3, 1, 2).reshape(block_rows, tree_len, -1)
    return (out_rows, max_rows, sum_rows)


def expert_rows(arrived, w_gate_up, w_down):
    exp_dev = w_gate_up.shape[0]
    sources = arrived.shape[0] // exp_dev
    grouped = arrived.reshape(sources, exp_dev, arrived.shape[1], arrived.shape[2])
    gate_proj = jnp.einsum(
        "sexd,edf->sexf", grouped, w_gate_up[:, 0], preferred_element_type=jnp.float32
    )
    upward = jnp.einsum(
        "sexd,edf->sexf", grouped, w_gate_up[:, 1], preferred_element_type=jnp.float32
    )
    active = (gate_proj * jax.nn.sigmoid(1.702 * gate_proj) * (upward + 1.0)).astype(jnp.bfloat16)
    down_part = jnp.einsum("sexf,efd->sexd", active, w_down, preferred_element_type=jnp.float32)
    return down_part.reshape(arrived.shape[0], arrived.shape[1], -1)


def shards(
    queries,
    draft_kv,
    cache_kv,
    cache_len,
    group_of,
    parents,
    sink_logit,
    w_out,
    hidden_in,
    norm_gain,
    routes,
    route_weight,
    w_gate_up,
    w_down,
    accepted_idx,
    accepted_len,
    tail_slot,
):
    seq_count = lax.axis_size("seq")
    req_dev, tree_len, head_cols = queries.shape
    kv_dev = cache_kv.shape[2]
    per_kv = HQ // KVH
    heads_dev = kv_dev * per_kv
    shard_len = cache_kv.shape[1]
    positions = lax.axis_index("seq") * shard_len + jnp.arange(shard_len, dtype=jnp.int32)
    every_query = lax.all_gather(queries, "seq", axis=0, tiled=True)
    requests_all = every_query.shape[0]
    block_count = requests_all // 8
    stacked = (
        every_query.reshape(block_count, 8, tree_len, head_cols),
        group_of.reshape(block_count, 8),
    )
    shard_out, shard_max, shard_sum = lax.map(
        lambda blocks: cache_block(blocks[0], blocks[1], cache_kv, cache_len, positions), stacked
    )
    shard_out = shard_out.reshape(seq_count, req_dev, tree_len, head_cols)
    shard_max = shard_max.reshape(seq_count, req_dev, tree_len, heads_dev)
    shard_sum = shard_sum.reshape(seq_count, req_dev, tree_len, heads_dev)
    came_out = lax.all_to_all(shard_out, "seq", split_axis=0, concat_axis=0, tiled=True)
    came_max, came_sum = (
        lax.all_to_all(shard_max, "seq", split_axis=0, concat_axis=0, tiled=True),
        lax.all_to_all(shard_sum, "seq", split_axis=0, concat_axis=0, tiled=True),
    )
    reachable = ancestry(parents)
    own_heads = queries.reshape(req_dev, tree_len, kv_dev, per_kv, HD)
    draft_keys = draft_kv[..., :HD]
    draft_values = draft_kv[..., HD:]
    tree_scores = (
        jnp.einsum("rtkqd,rukd->rkqtu", own_heads, draft_keys, preferred_element_type=jnp.float32)
        * 0.125
    )
    allowed = (reachable > 0.5)[:, None, None, :, :]
    tree_masked = jnp.where(allowed, tree_scores, -1e30)
    tree_max = jnp.max(tree_masked, axis=-1)
    tree_weight = jnp.where(allowed, jnp.exp(tree_masked - tree_max[..., None]), 0.0)
    tree_sum = jnp.sum(tree_weight, axis=-1)
    tree_num = jnp.einsum(
        "rkqtu,rukd->rkqtd",
        tree_weight.astype(jnp.bfloat16),
        draft_values,
        preferred_element_type=jnp.float32,
    )
    tree_max = tree_max.transpose(0, 3, 1, 2).reshape(req_dev, tree_len, heads_dev)
    tree_sum = tree_sum.transpose(0, 3, 1, 2).reshape(req_dev, tree_len, heads_dev)
    tree_num = tree_num.transpose(0, 3, 1, 2, 4).reshape(req_dev, tree_len, heads_dev, HD)
    sink_rows = sink_logit[None, None, :]
    ceiling = jnp.maximum(jnp.maximum(jnp.max(came_max, axis=0), tree_max), sink_rows)
    shard_scale = came_sum * jnp.exp(came_max - ceiling[None])
    tree_scale = jnp.exp(tree_max - ceiling)
    denominator = (
        jnp.sum(shard_scale, axis=0) + tree_scale * tree_sum + jnp.exp(sink_rows - ceiling)
    )
    weighted = jnp.sum(
        shard_scale[..., None]
        * came_out.reshape(seq_count, req_dev, tree_len, heads_dev, HD).astype(jnp.float32),
        axis=0,
    )
    numerator = weighted + tree_scale[..., None] * tree_num
    attention = (
        (numerator / denominator[..., None])
        .reshape(req_dev * tree_len, heads_dev * HD)
        .astype(jnp.bfloat16)
    )
    projected = jnp.dot(attention, w_out, preferred_element_type=jnp.float32)
    width_dev = hidden_in.shape[1]
    tp_index = lax.axis_index("tp")
    summed = lax.psum(projected, "tp")
    resid_full = lax.all_gather(hidden_in, "tp", axis=1, tiled=True)
    stream = (resid_full.astype(jnp.float32) + summed).astype(jnp.bfloat16)
    stream_f = stream.astype(jnp.float32)
    inv_scale = lax.rsqrt(jnp.mean(stream_f * stream_f, axis=-1, keepdims=True) + 1e-05)
    normed_full = (stream_f * inv_scale * norm_gain[None, :]).astype(jnp.bfloat16)
    stream_cols = lax.dynamic_slice_in_dim(stream, tp_index * width_dev, width_dev, 1)
    tok_dev = routes.shape[0]
    top_count = routes.shape[1]
    exp_dev = w_gate_up.shape[0]
    experts_all = seq_count * exp_dev
    capacity = 2 * tok_dev * top_count // experts_all
    flat_routes = routes.reshape(-1)
    onehot = (flat_routes[:, None] == jnp.arange(experts_all, dtype=jnp.int32)[None, :]).astype(
        jnp.int32
    )
    position = jnp.sum((jnp.cumsum(onehot, axis=0) - onehot) * onehot, axis=1)
    slot_ids = flat_routes * capacity + position
    buckets = jnp.arange(experts_all * capacity, dtype=jnp.int32)
    placing = jnp.sum(
        (slot_ids.reshape(tok_dev, top_count)[None, :, :] == buckets[:, None, None]).astype(
            jnp.int32
        ),
        axis=2,
    ).astype(jnp.bfloat16)
    dispatched = (
        jnp.dot(placing, normed_full, preferred_element_type=jnp.float32)
        .astype(jnp.bfloat16)
        .reshape(experts_all, capacity, -1)
    )
    down_part = expert_rows(
        lax.all_to_all(dispatched, "seq", split_axis=0, concat_axis=0, tiled=True),
        w_gate_up,
        w_down,
    )
    expert_out = lax.psum_scatter(
        down_part.astype(jnp.bfloat16), "tp", scatter_dimension=2, tiled=True
    )
    returned = lax.all_to_all(expert_out, "seq", split_axis=0, concat_axis=0, tiled=True)
    gathered_rows = jnp.take(
        returned.reshape(experts_all * capacity, -1), slot_ids, axis=0
    ).reshape(tok_dev, top_count, -1)
    mixture = jnp.sum(route_weight[:, :, None] * gathered_rows.astype(jnp.float32), axis=1)
    out_hidden = (stream_cols.astype(jnp.float32) + mixture).astype(jnp.bfloat16)
    blk_len = accepted_idx.shape[1]
    chosen = draft_kv[jnp.arange(req_dev, dtype=jnp.int32)[:, None], accepted_idx]
    kept_rows = jnp.arange(blk_len, dtype=jnp.int32)[None, :] < accepted_len[:, None]
    picked_rows = jnp.where(kept_rows[:, :, None, None], chosen, jnp.zeros_like(chosen))
    everyone = lax.all_gather(picked_rows, "seq", axis=0, tiled=True)
    my_slots = lax.axis_index("seq") * req_dev + jnp.arange(req_dev, dtype=jnp.int32)
    selector = (tail_slot[None, :] == my_slots[:, None]).astype(jnp.bfloat16)
    new_tail = jnp.dot(
        selector, everyone.reshape(everyone.shape[0], -1), preferred_element_type=jnp.float32
    ).astype(jnp.bfloat16)
    new_tail = new_tail.reshape(req_dev, blk_len, kv_dev, -1)
    return (out_hidden, new_tail)


def solution(mesh):
    in_specs = (
        P("seq", None, "tp"),
        P("seq", None, "tp", None),
        P(None, "seq", "tp", None),
        P(),
        P(),
        P("seq", None),
        P("tp"),
        P("tp", None),
        P("seq", "tp"),
        P(),
        P("seq", None),
        P("seq", None),
        P("seq", None, None, "tp"),
        P("seq", "tp", None),
        P("seq", None),
        P("seq"),
        P(),
    )
    out_specs = (P("seq", "tp"), P("seq", None, "tp", None))
    return jax.shard_map(shards, mesh=mesh, in_specs=in_specs, out_specs=out_specs, check_vma=False)
```

profile of v0, /device:TPU:1, one launch (start us, length us, event | category | flops | bytes accessed | tf_op | source)
XLA Modules:
  0.0 533.3 jit_solution(3878875501359007208)
XLA Ops:
  10.3 53.3 %all-gather.3.cloned.1.call-done = bf16[32,64,512]{2,1,0:T(8,128)(2,1)} async-done(((bf16[1,64,512]{2,1,0:T(8,128)(2,1)}), bf16[32,64,512]{2,1,0:T(8,128)(2,1)}) %all-gather.3.cloned.1.call-update) | async-done | bytes 2097168 | tf_op jit(solution)/shard_map/all_gather | solution.py:96
  63.7 97.3 %while.15 = (s32[]{:T(128)}, bf16[4,8,64,512]{3,2,1,0:T(8,128)(2,1)}, f32[4,8,64,8]{2,3,1,0:T(8,128)}, f32[4,8,64,8]{2,3,1,0:T(8,128)}, s32[4,8]{1,0:T(4,128)S(1...) while((s32[]{:T(128)}, ...), condition=%wide.region_3.4_spmd.clone, body=%wide.region_0.3_spmd.clone.sunk | while | flops 565184128 | bytes 43791872 | solution.py:103
  65.0 2.9 gather_fusion.1
  67.9 2.3 copy.129
  70.2 2.4 bitcast_select_fusion.4
  75.3 2.7 bitcast_reduce_fusion.3
  78.0 2.3 fusion.128
  80.9 2.6 fusion.129
  89.4 2.9 gather_fusion.1
  92.3 2.3 copy.129
  94.5 2.4 bitcast_select_fusion.4
  99.6 2.7 bitcast_reduce_fusion.3
  102.3 2.3 fusion.128
  105.3 2.6 fusion.129
  113.7 2.9 gather_fusion.1
  116.6 2.3 copy.129
  118.9 2.4 bitcast_select_fusion.4
  124.0 2.7 bitcast_reduce_fusion.3
  126.7 2.3 fusion.128
  129.6 2.6 fusion.129
  138.0 2.9 gather_fusion.1
  143.2 2.4 bitcast_select_fusion.4
  148.3 2.7 bitcast_reduce_fusion.3
  151.0 2.3 fusion.128
  153.9 2.6 fusion.129
  162.7 5.1 all-to-all-start.1
  170.4 4.7 all-to-all-done.1
  175.1 3.9 all-to-all-start
  180.8 5.6 %all-to-all-done = f32[32,1,512]{2,1,0:T(1,128)S(1)} async-done(((f32[32,1,512]{2,1,0:T(1,128)}), f32[32,1,512]{2,1,0:T(1,128)S(1)}, u32[]{:S(2)}, u32[]{:S(2)}) %all-to-all-start) | async-done | bytes 65568 | tf_op jit(solution)/shard_map/all_to_all | solution.py:112
  186.4 4.7 all-to-all-start.2
  193.3 23.3 %all-gather = bf16[8,360,64]{1,2,0:T(8,128)(2,1)S(1)} all-gather(bf16[1,360,64]{1,2,0:T(8,128)(2,1)} %bitcast.318), channel_id=1, replica_groups=mesh['seq'=32,'tp'=8] {'tp'}, dimensions={0}, use_global_device_ids=true | all-gather | bytes 414720 | tf_op jit(solution)/shard_map/all_gather | solution.py:158
  227.4 5.9 %mul.135 = f32[32,64,8,64]{3,2,1,0:T(8,128)} broadcast(f32[32,64,8]{2,1,0:T(8,128)} %copy.92), dimensions={0,1,2} | broadcast | bytes 4259840 | tf_op jit(solution)/shard_map/mul | solution.py:144
  233.4 7.5 %mul.136 = f32[32,1,64,512]{3,2,1,0:T(8,128)} reshape(f32[32,64,8,64]{3,2,1,0:T(8,128)} %mul.135) | data formatting | bytes 8388608 | tf_op jit(solution)/shard_map/mul | solution.py:144
  240.9 3.6 multiply_reduce_fusion
  247.8 72.6 %all-reduce.3.cloned.1.call-done = f32[64,2880]{1,0:T(8,128)} async-done(((f32[64,2880]{1,0:T(8,128)}), f32[64,2880]{1,0:T(8,128)}) %all-reduce.3.cloned.1.call-update) | async-done | bytes 737296 | tf_op jit(solution)/shard_map/psum | solution.py:157
  322.7 2.7 convolution_convert_fusion.1
  325.4 4.6 copy.103
  329.9 50.3 %all_to_all.25 = bf16[32,16,2880]{2,1,0:T(8,128)(2,1)S(1)} all-to-all(bf16[32,16,2880]{2,1,0:T(8,128)(2,1)} %bitcast.309), channel_id=1, replica_groups=mesh['seq'=32,'tp'=8] {'seq'}, dimensions={0} | all-to-all | bytes 5898240 | tf_op jit(solution)/shard_map/all_to_all | solution.py:188
  381.9 4.2 fusion.27
  386.1 8.5 %convolution_convert_fusion = bf16[32,16,2880]{2,1,0:T(8,128)(2,1)} fusion(bf16[1,360,2880]{2,1,0:T(8,128)(2,1)} %param.32, bf16[32,16,2880]{2,1,0:T(8,128)(2,1)} %copy-done.2, bf16[1,2,2880,360]{2,3,1,0:T(8,128)(2,1)} %param.31, f32[32,1,16,360]{3,2,0,1:T(8,128)} %fusion.27), kind=kOutput, calls=%fused_computation.40 | convolution fusion | flops 2126315520 | bytes 10989568 | tf_op jit(solution)/shard_map/sexf,efd->sexd/dot_general | solution.py:66
  394.6 21.4 %copy.108 = bf16[32,16,2880]{1,0,2:T(8,128)(2,1)} copy(bf16[32,16,2880]{2,1,0:T(8,128)(2,1)} %convolution_convert_fusion) | data formatting | bytes 5898240
  416.0 39.5 %reshape.749 = bf16[2880,512]{1,0:T(8,128)(2,1)} reshape(bf16[2880,32,16]{2,1,0:T(8,128)(2,1)} %bitcast.306) | data formatting | bytes 5898240
  457.1 22.6 %all_gather.11 = bf16[32,16,1,128]{3,1,2,0:T(8,128)(2,1)S(1)} all-gather(bf16[1,16,1,128]{3,1,2,0:T(8,128)(2,1)S(1)} %bitcast_select_fusion.2), channel_id=1, replica_groups=mesh['seq'=32,'tp'=8] {'seq'}, dimensions={0}, use_global_device_ids=true | all-gather | bytes 135168 | tf_op jit(solution)/shard_map/all_gather | solution.py:205
  479.9 12.3 %reduce-scatter.4.cloned.1.call-done = bf16[360,512]{1,0:T(8,128)(2,1)} async-done(((bf16[2880,512]{1,0:T(8,128)(2,1)}), bf16[360,512]{1,0:T(8,128)(2,1)}) %reduce-scatter.4.cloned.1.call-update) | async-done | bytes 368656
  492.2 4.4 reshape.750
  496.5 5.0 copy.109
  501.6 11.1 %all-to-all-start.4 = ((bf16[32,16,360]{2,1,0:T(8,128)(2,1)}), bf16[32,16,360]{2,1,0:T(8,128)(2,1)S(1)}, u32[]{:S(2)}, u32[]{:S(2)}) async-start(bf16[32,16,360]{2,1,0:T(8,128)(2,1)} %copy.109), calls=%async_computation.4 | async-start | bytes 786432 | tf_op jit(solution)/shard_map/all_to_all | solution.py:195
  514.1 8.7 %all-to-all-done.4 = bf16[32,16,360]{2,1,0:T(8,128)(2,1)S(1)} async-done(((bf16[32,16,360]{2,1,0:T(8,128)(2,1)}), bf16[32,16,360]{2,1,0:T(8,128)(2,1)S(1)}, u32[]{:S(2)}, u32[]{:S(2)}) %all-to-all-start.4) | async-done | bytes 368672 | tf_op jit(solution)/shard_map/all_to_all | solution.py:195
  (178 shorter events, 74.3 us)
Async XLA Ops:
  7.2 237.3 %copy-start = (bf16[512,2880]{0,1:T(8,128)(2,1)S(1)}, bf16[512,2880]{0,1:T(8,128)(2,1)}, u32[]{:S(2)}) copy-start(bf16[512,2880]{0,1:T(8,128)(2,1)} %param.26) | copy-start | bytes 8847364
  7.2 56.5 %all-gather.3.cloned.1.call-start = ((), (), s32[]{:S(2)}) async-start(), calls=%async_computation.6 | async-start | bytes 2162688 | tf_op jit(solution)/shard_map/all_gather | solution.py:96
  63.7 115.5 %copy-start.6 = (bf16[1,64,512]{2,1,0:T(8,128)(2,1)S(1)}, bf16[1,64,512]{2,1,0:T(8,128)(2,1)}, u32[]{:S(2)}) copy-start(bf16[1,64,512]{2,1,0:T(8,128)(2,1)} %param.19) | copy-start | bytes 196612
  63.7 115.6 %copy-start.13 = (s32[64,4]{0,1:T(4,128)S(1)}, s32[64,4]{0,1:T(4,128)}, u32[]{:S(2)}) copy-start(s32[64,4]{0,1:T(4,128)} %param.29) | copy-start | bytes 3076
  78.0 3.0 copy-start.1
  102.3 3.0 copy-start.1
  126.6 3.0 copy-start.1
  150.9 3.0 copy-start.1
  161.0 30.9 %copy-start.7 = (bf16[1,64,1,128]{3,1,2,0:T(8,128)(2,1)S(1)}, bf16[1,64,1,128]{3,1,2,0:T(8,128)(2,1)}, u32[]{:S(2)}) copy-start(bf16[1,64,1,128]{3,1,2,0:T(8,128)(2,1)} %param.20) | copy-start | bytes 49156
  162.7 12.4 %all-to-all-start.1 = ((f32[32,1,512]{2,1,0:T(1,128)}), f32[32,1,512]{2,1,0:T(1,128)S(1)}, u32[]{:S(2)}, u32[]{:S(2)}) async-start(f32[32,1,512]{2,1,0:T(1,128)} %reshape.754), calls=%async_computation.1 | async-start | bytes 131072 | tf_op jit(solution)/shard_map/all_to_all | solution.py:111
  175.1 17.0 %copy-start.9 = (f32[32,1,512]{2,1,0:T(1,128)}, f32[32,1,512]{2,1,0:T(1,128)S(1)}, u32[]{:S(2)}) copy-start(f32[32,1,512]{2,1,0:T(1,128)S(1)} %all-to-all-done.1) | copy-start | bytes 196612
  175.1 11.3 %all-to-all-start = ((f32[32,1,512]{2,1,0:T(1,128)}), f32[32,1,512]{2,1,0:T(1,128)S(1)}, u32[]{:S(2)}, u32[]{:S(2)}) async-start(f32[32,1,512]{2,1,0:T(1,128)} %reshape.752), calls=%async_computation | async-start | bytes 131072 | tf_op jit(solution)/shard_map/all_to_all | solution.py:112
  186.4 4.8 copy-start.11
  186.4 54.4 %all-to-all-start.2 = ((bf16[32,1,64,512]{3,2,1,0:T(8,128)(2,1)}), bf16[32,1,64,512]{3,2,1,0:T(8,128)(2,1)}, u32[]{:S(2)}, u32[]{:S(2)}) async-start(bf16[32,1,64,512]{3,2,1,0:T(8,128)(2,1)} %bitcast.313), calls=%async_computation.2 | async-start | bytes 4194304 | tf_op jit(solution)/shard_map/all_to_all | solution.py:109
  191.2 129.2 %all-reduce.3.cloned.1.call-start = ((), (), s32[]{:S(2)}) async-start(), calls=%async_computation.7 | async-start | bytes 1507328 | tf_op jit(solution)/shard_map/psum | solution.py:157
  192.4 28.8 %copy-start.10 = (f32[32,1,512]{2,1,0:T(1,128)S(1)}, f32[32,1,512]{2,1,0:T(1,128)}, u32[]{:S(2)}) copy-start(f32[32,1,512]{2,1,0:T(1,128)} %copy-done.9) | copy-start | bytes 196612
  193.3 28.8 %copy-start.12 = (f32[32,1,512]{2,1,0:T(1,128)S(1)}, f32[32,1,512]{2,1,0:T(1,128)}, u32[]{:S(2)}) copy-start(f32[32,1,512]{2,1,0:T(1,128)} %copy-done.11) | copy-start | bytes 196612
  240.9 3.6 copy-start.4
  240.9 3.6 copy-start.5
  244.5 2.0 copy-start.16
  244.5 2.8 copy-start.15
  244.5 78.2 %copy-start.14 = (f32[2880]{0:T(1024)S(1)}, f32[2880]{0:T(1024)}, u32[]{:S(2)}) copy-start(f32[2880]{0:T(1024)} %param.28) | copy-start | bytes 34564
  246.4 245.7 %reduce-scatter.4.cloned.1.call-start = ((), (), s32[]{:S(2)}) async-start(), calls=%async_computation.8 | async-start | bytes 3317760
  321.9 0.8 copy-start.3
  380.2 1.6 copy-start.2
  455.4 0.9 copy-start.19
  455.4 1.0 copy-start.8
  455.4 24.3 %copy-start.18 = (s32[32]{0:T(128)S(1)}, s32[32]{0:T(128)}, u32[]{:S(2)}) copy-start(s32[32]{0:T(128)} %param.35) | copy-start | bytes 388
  479.8 33.0 %copy-start.17 = (f32[64,4]{0,1:T(4,128)S(1)}, f32[64,4]{0,1:T(4,128)}, u32[]{:S(2)}) copy-start(f32[64,4]{0,1:T(4,128)} %param.30) | copy-start | bytes 3076
  501.6 21.3 %all-to-all-start.4 = ((bf16[32,16,360]{2,1,0:T(8,128)(2,1)}), bf16[32,16,360]{2,1,0:T(8,128)(2,1)S(1)}, u32[]{:S(2)}, u32[]{:S(2)}) async-start(bf16[32,16,360]{2,1,0:T(8,128)(2,1)} %copy.109), calls=%async_computation.4 | async-start | bytes 786432 | tf_op jit(solution)/shard_map/all_to_all | solution.py:195
Sparse Core Ops, SparseCore 0:
  10.6 53.0 all-gather.2
  246.5 73.8 all-reduce.2
  455.6 36.5 reduce-scatter.3
where the time goes:
time: 536 us; the launch traced here: 533 us
  local copies, waits for them, and re-layouts  164 us (31%)
  waiting for transfers between devices  158 us (29%)
  blocking collectives  96.2 us (18%)
  matrix products  42.4 us (8%)
  other arithmetic  32.4 us (6%)
  starting transfers between devices  25 us (5%)
  between operations  14.9 us (3%)
    unnamed x48, local copies, waits for them, and re-layouts  77 us
    psum x1, waiting for transfers between devices, shards(): summed = lax.psum(projected, 'tp')  72.6 us
    all_gather x1, waiting for transfers between devices, shards(): every_query = lax.all_gather(queries, 'seq', axis=0, tiled=True)  53.3 us
    all_to_all x1, blocking collectives, shards(): lax.all_to_all(dispatched, 'seq', split_axis=0, concat_axis=0, tiled=True)  50.3 us
    all_gather x1, blocking collectives, shards(): resid_full = lax.all_gather(hidden_in, 'tp', axis=1, tiled=True)  23.3 us
    all_gather x1, blocking collectives, shards(): everyone = lax.all_gather(picked_rows, 'seq', axis=0, tiled=True)  22.6 us
    gather x8, local copies, waits for them, and re-layouts, cache_block(): picked = jnp.take(cache_kv, block_groups, axis=0)  20.7 us
    mul x3, local copies, waits for them, and re-layouts, shards(): shard_scale[..., None]  14.9 us
  transfers between devices with their start and end apart: 7, of which 6 were waited for; matrix products, arithmetic and copies ran while one was open for 7% of the time, Pallas kernels for 0%

commit v1 on v0

--- a/solution.py
+++ b/solution.py
@@ -6,6 +6,21 @@
 HQ = 64
 KVH = 8
 HD = 64
+
+
+def settle_the_zones(axis_name, local):
+    n_all = lax.psum(1, axis_name)
+    frame_out = [(hop_no - 1, hop_no) for hop_no in range(1, n_all)] + [(n_all - 1, 0)]
+    new = local
+    cards = [new]
+    for _ in tuple(range(n_all - 1)):
+        new = lax.ppermute(new, axis_name, frame_out)
+        cards += [new]
+    return jnp.roll(
+        jnp.concatenate([*reversed(cards)], axis=1),
+        (lax.axis_index(axis_name) + 1) * new.shape[1],
+        axis=1,
+    )
 
 
 def ancestry(parents):
@@ -155,7 +170,7 @@
     width_dev = hidden_in.shape[1]
     tp_index = lax.axis_index("tp")
     summed = lax.psum(projected, "tp")
-    resid_full = lax.all_gather(hidden_in, "tp", axis=1, tiled=True)
+    resid_full = settle_the_zones("tp", hidden_in)
     stream = (resid_full.astype(jnp.float32) + summed).astype(jnp.bfloat16)
     stream_f = stream.astype(jnp.float32)
     inv_scale = lax.rsqrt(jnp.mean(stream_f * stream_f, axis=-1, keepdims=True) + 1e-05)

time: 536 us -> 513 us (0.957)
  blocking collectives: 96.2 us -> 72.9 us
    all_gather x1 -> x0, blocking collectives: 23.3 us -> none  [shards(): resid_full = lax.all_gather(hidden_in, 'tp', axis=1, tiled=True)]
    psum x1, waiting for transfers between devices: 72.6 us -> 51.6 us  [shards(): summed = lax.psum(projected, 'tp')]
    ppermute x0 -> x7, waiting for transfers between devices: none -> 19.1 us  [settle_the_zones(): new = lax.ppermute(new, axis_name, frame_out)]
    unnamed x48 -> x40, local copies, waits for them, and re-layouts: 77 us -> 77 us
  transfers between devices with their start and end apart: 7 -> 14, of which waited for: 6 -> 11; matrix products, arithmetic and copies ran while one was open for 7% -> 27% of each run, Pallas kernels for 0% -> 0%
where the time goes in v1:
time: 513 us; the launch traced here: 511 us
  local copies, waits for them, and re-layouts  163 us (32%)
  waiting for transfers between devices  158 us (31%)
  blocking collectives  72.9 us (14%)
  matrix products  40.2 us (8%)
  other arithmetic  31.5 us (6%)
  starting transfers between devices  30 us (6%)
  between operations  14.8 us (3%)
    unnamed x40, local copies, waits for them, and re-layouts  77 us
    all_gather x1, waiting for transfers between devices, shards(): every_query = lax.all_gather(queries, 'seq', axis=0, tiled=True)  52.5 us
    psum x1, waiting for transfers between devices, shards(): summed = lax.psum(projected, 'tp')  51.6 us
    all_to_all x1, blocking collectives, shards(): lax.all_to_all(dispatched, 'seq', split_axis=0, concat_axis=0, tiled=True)  50.3 us
    all_gather x1, blocking collectives, shards(): everyone = lax.all_gather(picked_rows, 'seq', axis=0, tiled=True)  22.6 us
    gather x8, local copies, waits for them, and re-layouts, cache_block(): picked = jnp.take(cache_kv, block_groups, axis=0)  20.7 us
    ppermute x7, waiting for transfers between devices, settle_the_zones(): new = lax.ppermute(new, axis_name, frame_out)  19.1 us
    mul x3, local copies, waits for them, and re-layouts, shards(): shard_scale[..., None]  15.8 us
  transfers between devices with their start and end apart: 14, of which 11 were waited for; matrix products, arithmetic and copies ran while one was open for 27% of the time, Pallas kernels for 0%

profile of v1, /device:TPU:1, one launch (start us, length us, event | category | flops | bytes accessed | tf_op | source)
XLA Modules:
  0.0 510.7 jit_solution(6322982661219075779)
XLA Ops:
  7.9 2.5 collective-permute-start
  11.2 52.5 %all-gather.2.cloned.1.call-done = bf16[32,64,512]{2,1,0:T(8,128)(2,1)} async-done(((bf16[1,64,512]{2,1,0:T(8,128)(2,1)}), bf16[32,64,512]{2,1,0:T(8,128)(2,1)}) %all-gather.2.cloned.1.call-update) | async-done | bytes 2097168 | tf_op jit(solution)/shard_map/all_gather | solution.py:111
  63.7 97.3 %while.15 = (s32[]{:T(128)}, bf16[4,8,64,512]{3,2,1,0:T(8,128)(2,1)}, f32[4,8,64,8]{2,3,1,0:T(8,128)}, f32[4,8,64,8]{2,3,1,0:T(8,128)}, s32[4,8]{1,0:T(4,128)S(1...) while((s32[]{:T(128)}, ...), condition=%wide.region_3.4_spmd.clone, body=%wide.region_0.3_spmd.clone.sunk | while | flops 565184128 | bytes 43791872 | solution.py:118
  65.0 2.9 gather_fusion.1
  70.2 2.4 bitcast_select_fusion.4
  75.3 2.7 bitcast_reduce_fusion.3
  78.0 2.3 fusion.126
  80.9 2.6 fusion.127
  89.4 2.9 gather_fusion.1
  94.5 2.4 bitcast_select_fusion.4
  99.6 2.7 bitcast_reduce_fusion.3
  105.3 2.6 fusion.127
  113.7 2.9 gather_fusion.1
  118.9 2.4 bitcast_select_fusion.4
  123.9 2.7 bitcast_reduce_fusion.3
  129.6 2.6 fusion.127
  138.0 2.9 gather_fusion.1
  143.2 2.4 bitcast_select_fusion.4
  148.2 2.7 bitcast_reduce_fusion.3
  153.9 2.6 fusion.127
  162.7 5.1 %all-to-all-start.1 = ((f32[32,1,512]{2,1,0:T(1,128)}), f32[32,1,512]{2,1,0:T(1,128)S(1)}, u32[]{:S(2)}, u32[]{:S(2)}) async-start(f32[32,1,512]{2,1,0:T(1,128)} %reshape.751), calls=%async_computation.1 | async-start | bytes 131072 | tf_op jit(solution)/shard_map/all_to_all | solution.py:126
  169.7 5.5 %all-to-all-done.1 = f32[32,1,512]{2,1,0:T(1,128)S(1)} async-done(((f32[32,1,512]{2,1,0:T(1,128)}), f32[32,1,512]{2,1,0:T(1,128)S(1)}, u32[]{:S(2)}, u32[]{:S(2)}) %all-to-all-start.1) | async-done | bytes 65568 | tf_op jit(solution)/shard_map/all_to_all | solution.py:126
  175.1 3.9 all-to-all-start
  179.2 7.3 %all-to-all-done = f32[32,1,512]{2,1,0:T(1,128)S(1)} async-done(((f32[32,1,512]{2,1,0:T(1,128)}), f32[32,1,512]{2,1,0:T(1,128)S(1)}, u32[]{:S(2)}, u32[]{:S(2)}) %all-to-all-start) | async-done | bytes 65568 | tf_op jit(solution)/shard_map/all_to_all | solution.py:127
  186.4 4.9 all-to-all-start.2
  195.3 2.7 collective-permute-done.1
  203.7 2.3 copy.87
  206.0 5.9 %mul.139 = f32[32,64,8,64]{3,2,1,0:T(8,128)} broadcast(f32[32,64,8]{2,1,0:T(8,128)} %copy.87), dimensions={0,1,2} | broadcast | bytes 4259840 | tf_op jit(solution)/shard_map/mul | solution.py:159
  212.0 7.5 %mul.140 = f32[32,1,64,512]{3,2,1,0:T(8,128)} reshape(f32[32,64,8,64]{3,2,1,0:T(8,128)} %mul.139) | data formatting | bytes 8388608 | tf_op jit(solution)/shard_map/mul | solution.py:159
  219.5 3.6 multiply_reduce_fusion
  227.1 3.1 collective-permute-done.3
  230.5 3.9 collective-permute-done.4
  234.4 4.2 collective-permute-done.5
  238.8 5.1 %collective-permute-done.6 = bf16[64,360]{1,0:T(8,128)(2,1)S(1)} collective-permute-done((bf16[64,360]{1,0:T(8,128)(2,1)S(1)}, bf16[64,360]{1,0:T(8,128)(2,1)S(1)}, u32[]{:S(2)}, u32[]{:S(2)}) %collective-permute-start.6) | collective-permute-done | bytes 46112 | tf_op jit(solution)/shard_map/ppermute | solution.py:17
  246.1 51.6 %all-reduce.3.cloned.1.call-done = f32[64,2880]{1,0:T(8,128)} async-done(((f32[64,2880]{1,0:T(8,128)}), f32[64,2880]{1,0:T(8,128)}) %all-reduce.3.cloned.1.call-update) | async-done | bytes 737296 | tf_op jit(solution)/shard_map/psum | solution.py:172
  300.0 2.7 convolution_convert_fusion.1
  302.7 4.6 copy.98
  307.2 50.3 %all_to_all.25 = bf16[32,16,2880]{2,1,0:T(8,128)(2,1)S(1)} all-to-all(bf16[32,16,2880]{2,1,0:T(8,128)(2,1)} %bitcast.299), channel_id=1, replica_groups=mesh['seq'=32,'tp'=8] {'seq'}, dimensions={0} | all-to-all | bytes 5898240 | tf_op jit(solution)/shard_map/all_to_all | solution.py:203
  359.1 4.2 fusion.27
  363.4 8.5 %convolution_convert_fusion = bf16[32,16,2880]{2,1,0:T(8,128)(2,1)} fusion(bf16[1,360,2880]{2,1,0:T(8,128)(2,1)} %param.32, bf16[32,16,2880]{2,1,0:T(8,128)(2,1)} %copy-done.2, bf16[1,2,2880,360]{2,3,1,0:T(8,128)(2,1)} %param.31, f32[32,1,16,360]{3,2,0,1:T(8,128)} %fusion.27), kind=kOutput, calls=%fused_computation.40 | convolution fusion | flops 2126315520 | bytes 10989568 | tf_op jit(solution)/shard_map/sexf,efd->sexd/dot_general | solution.py:81
  371.9 21.4 %copy.103 = bf16[32,16,2880]{1,0,2:T(8,128)(2,1)} copy(bf16[32,16,2880]{2,1,0:T(8,128)(2,1)} %convolution_convert_fusion) | data formatting | bytes 5898240
  393.2 39.5 %reshape.746 = bf16[2880,512]{1,0:T(8,128)(2,1)} reshape(bf16[2880,32,16]{2,1,0:T(8,128)(2,1)} %bitcast.296) | data formatting | bytes 5898240
  434.4 22.6 %all_gather.7 = bf16[32,16,1,128]{3,1,2,0:T(8,128)(2,1)S(1)} all-gather(bf16[1,16,1,128]{3,1,2,0:T(8,128)(2,1)S(1)} %bitcast_select_fusion.2), channel_id=1, replica_groups=mesh['seq'=32,'tp'=8] {'seq'}, dimensions={0}, use_global_device_ids=true | all-gather | bytes 135168 | tf_op jit(solution)/shard_map/all_gather | solution.py:220
  457.1 12.5 %reduce-scatter.4.cloned.1.call-done = bf16[360,512]{1,0:T(8,128)(2,1)} async-done(((bf16[2880,512]{1,0:T(8,128)(2,1)}), bf16[360,512]{1,0:T(8,128)(2,1)}) %reduce-scatter.4.cloned.1.call-update) | async-done | bytes 368656
  469.6 4.4 reshape.747
  474.0 5.0 copy.104
  479.0 11.0 %all-to-all-start.4 = ((bf16[32,16,360]{2,1,0:T(8,128)(2,1)}), bf16[32,16,360]{2,1,0:T(8,128)(2,1)S(1)}, u32[]{:S(2)}, u32[]{:S(2)}) async-start(bf16[32,16,360]{2,1,0:T(8,128)(2,1)} %copy.104), calls=%async_computation.4 | async-start | bytes 786432 | tf_op jit(solution)/shard_map/all_to_all | solution.py:210
  491.5 8.7 %all-to-all-done.4 = bf16[32,16,360]{2,1,0:T(8,128)(2,1)S(1)} async-done(((bf16[32,16,360]{2,1,0:T(8,128)(2,1)}), bf16[32,16,360]{2,1,0:T(8,128)(2,1)S(1)}, u32[]{:S(2)}, u32[]{:S(2)}) %all-to-all-start.4) | async-done | bytes 368672 | tf_op jit(solution)/shard_map/all_to_all | solution.py:210
  (182 shorter events, 84.1 us)
Async XLA Ops:
  7.2 215.9 %copy-start = (bf16[512,2880]{0,1:T(8,128)(2,1)S(1)}, bf16[512,2880]{0,1:T(8,128)(2,1)}, u32[]{:S(2)}) copy-start(bf16[512,2880]{0,1:T(8,128)(2,1)} %param.26) | copy-start | bytes 8847364
  7.2 56.5 %all-gather.2.cloned.1.call-start = ((), (), s32[]{:S(2)}) async-start(), calls=%async_computation.6 | async-start | bytes 2162688 | tf_op jit(solution)/shard_map/all_gather | solution.py:111
  7.9 184.9 %collective-permute-start = (bf16[64,360]{1,0:T(8,128)(2,1)}, bf16[64,360]{1,0:T(8,128)(2,1)}, u32[]{:S(2)}, u32[]{:S(2)}) collective-permute-start(bf16[64,360]{1,0:T(8,128)(2,1)} %param.27), channel_id=1, source_target_pairs={{0,1},{1,2},{2,3},{3,4},{4,5},{5,6},{6,7},{7,0},{8,9},{9,10},{10,1... | collective-permute-start | bytes 138248 | tf_op jit(solution)/shard_map/ppermute | solution.py:17
  63.7 104.1 %copy-start.14 = (s32[1,64]{1,0:T(1,128)S(1)}, s32[1,64]{1,0:T(1,128)}, u32[]{:S(2)}) copy-start(s32[1,64]{1,0:T(1,128)} %param.24) | copy-start | bytes 772
  78.0 3.0 copy-start.1
  102.3 3.0 copy-start.1
  126.6 3.0 copy-start.1
  150.9 3.0 copy-start.1
  161.0 30.6 %copy-start.5 = (bf16[1,64,512]{2,1,0:T(8,128)(2,1)S(1)}, bf16[1,64,512]{2,1,0:T(8,128)(2,1)}, u32[]{:S(2)}) copy-start(bf16[1,64,512]{2,1,0:T(8,128)(2,1)} %param.19) | copy-start | bytes 196612
  161.0 31.3 %copy-start.6 = (bf16[1,64,1,128]{3,1,2,0:T(8,128)(2,1)S(1)}, bf16[1,64,1,128]{3,1,2,0:T(8,128)(2,1)}, u32[]{:S(2)}) copy-start(bf16[1,64,1,128]{3,1,2,0:T(8,128)(2,1)} %param.20) | copy-start | bytes 49156
  162.7 12.5 %all-to-all-start.1 = ((f32[32,1,512]{2,1,0:T(1,128)}), f32[32,1,512]{2,1,0:T(1,128)S(1)}, u32[]{:S(2)}, u32[]{:S(2)}) async-start(f32[32,1,512]{2,1,0:T(1,128)} %reshape.751), calls=%async_computation.1 | async-start | bytes 131072 | tf_op jit(solution)/shard_map/all_to_all | solution.py:126
  175.1 11.3 %all-to-all-start = ((f32[32,1,512]{2,1,0:T(1,128)}), f32[32,1,512]{2,1,0:T(1,128)S(1)}, u32[]{:S(2)}, u32[]{:S(2)}) async-start(f32[32,1,512]{2,1,0:T(1,128)} %reshape.749), calls=%async_computation | async-start | bytes 131072 | tf_op jit(solution)/shard_map/all_to_all | solution.py:127
  186.4 8.1 %copy-start.7 = (s32[64,4]{0,1:T(4,128)S(1)}, s32[64,4]{0,1:T(4,128)}, u32[]{:S(2)}) copy-start(s32[64,4]{0,1:T(4,128)} %param.29) | copy-start | bytes 3076
  186.4 13.9 %copy-start.12 = (f32[8]{0:T(128)S(1)}, f32[8]{0:T(128)}, u32[]{:S(2)}) copy-start(f32[8]{0:T(128)} %param.25) | copy-start | bytes 100
  186.4 33.0 %all-to-all-start.2 = ((bf16[32,1,64,512]{3,2,1,0:T(8,128)(2,1)}), bf16[32,1,64,512]{3,2,1,0:T(8,128)(2,1)}, u32[]{:S(2)}, u32[]{:S(2)}) async-start(bf16[32,1,64,512]{3,2,1,0:T(8,128)(2,1)} %bitcast.303), calls=%async_computation.2 | async-start | bytes 4194304 | tf_op jit(solution)/shard_map/all_to_all | solution.py:124
  191.3 106.4 %all-reduce.3.cloned.1.call-start = ((), (), s32[]{:S(2)}) async-start(), calls=%async_computation.7 | async-start | bytes 1507328 | tf_op jit(solution)/shard_map/psum | solution.py:172
  192.8 5.2 %collective-permute-start.1 = (bf16[64,360]{1,0:T(8,128)(2,1)}, bf16[64,360]{1,0:T(8,128)(2,1)}, u32[]{:S(2)}, u32[]{:S(2)}) collective-permute-start(bf16[64,360]{1,0:T(8,128)(2,1)} %collective-permute-done), channel_id=1, source_target_pairs={{0,1},{1,2},{2,3},{3,4},{4,5},{5,6},{6,7},{7,0},{8,9},{9,10},{10,1... | collective-permute-start | bytes 138248 | tf_op jit(solution)/shard_map/ppermute | solution.py:17
  198.0 27.7 %collective-permute-start.2 = (bf16[64,360]{1,0:T(8,128)(2,1)}, bf16[64,360]{1,0:T(8,128)(2,1)}, u32[]{:S(2)}, u32[]{:S(2)}) collective-permute-start(bf16[64,360]{1,0:T(8,128)(2,1)} %collective-permute-done.1), channel_id=1, source_target_pairs={{0,1},{1,2},{2,3},{3,4},{4,5},{5,6},{6,7},{7,0},{8,9},{9,10},{10,1... | collective-permute-start | bytes 138248 | tf_op jit(solution)/shard_map/ppermute | solution.py:17
  219.4 3.6 copy-start.4
  223.0 2.0 copy-start.10
  223.1 11.3 %copy-start.8 = (s32[64,4]{0,1:T(4,128)S(1)}, s32[64,4]{0,1:T(4,128)}, u32[]{:S(2)}) copy-start(s32[64,4]{0,1:T(4,128)} %param.29) | copy-start | bytes 3076
  225.0 75.0 %copy-start.9 = (f32[2880]{0:T(1024)S(1)}, f32[2880]{0:T(1024)}, u32[]{:S(2)}) copy-start(f32[2880]{0:T(1024)} %param.28) | copy-start | bytes 34564
  225.0 244.6 %reduce-scatter.4.cloned.1.call-start = ((), (), s32[]{:S(2)}) async-start(), calls=%async_computation.8 | async-start | bytes 3317760
  225.7 4.6 collective-permute-start.3
  230.2 4.2 collective-permute-start.4
  234.4 4.3 collective-permute-start.5
  238.6 5.3 %collective-permute-start.6 = (bf16[64,360]{1,0:T(8,128)(2,1)S(1)}, bf16[64,360]{1,0:T(8,128)(2,1)S(1)}, u32[]{:S(2)}, u32[]{:S(2)}) collective-permute-start(bf16[64,360]{1,0:T(8,128)(2,1)S(1)} %collective-permute-done.5), channel_id=1, source_target_pairs={{0,1},{1,2},{2,3},{3,4},{4,5},{5,6},{6,7},{7,0},{8,9},{9,10},{10,1... | collective-permute-start | bytes 138248 | tf_op jit(solution)/shard_map/ppermute | solution.py:17
  299.2 0.8 copy-start.3
  357.5 1.6 copy-start.2
  432.7 0.9 copy-start.15
  432.7 24.2 %copy-start.13 = (s32[32]{0:T(128)S(1)}, s32[32]{0:T(128)}, u32[]{:S(2)}) copy-start(s32[32]{0:T(128)} %param.35) | copy-start | bytes 388
  457.1 33.1 %copy-start.11 = (f32[64,4]{0,1:T(4,128)S(1)}, f32[64,4]{0,1:T(4,128)}, u32[]{:S(2)}) copy-start(f32[64,4]{0,1:T(4,128)} %param.30) | copy-start | bytes 3076
  479.0 21.2 %all-to-all-start.4 = ((bf16[32,16,360]{2,1,0:T(8,128)(2,1)}), bf16[32,16,360]{2,1,0:T(8,128)(2,1)S(1)}, u32[]{:S(2)}, u32[]{:S(2)}) async-start(bf16[32,16,360]{2,1,0:T(8,128)(2,1)} %copy.104), calls=%async_computation.4 | async-start | bytes 786432 | tf_op jit(solution)/shard_map/all_to_all | solution.py:210
Sparse Core Ops, SparseCore 0:
  10.6 53.0 all-gather.1
  225.1 72.5 all-reduce.2
  432.9 36.7 reduce-scatter.3
